TPU v7x, 512 devices: a whole 4x4x16 slice. The times are simulated.
512 devices in a mesh: blk: 8 (over x, z_hi), grp: 64 (over y, z_lo, core).
Axes of the slice: x: 4, y: 4, z: 16 (z_hi: 2, z_lo: 8; z = z_hi * 8 + z_lo), core: 2. Of those that a mesh axis runs over, the one named last changes fastest.
Arguments:
- images: bfloat16 [8192, 1152], P(('blk', 'grp')), may hold values from -6 to 6
- texts: bfloat16 [8192, 1152], P(('blk', 'grp')), may hold values from -6 to 6
- scale: float32 [], replicated, may hold values from 8 to 16
- shift: float32 [], replicated, may hold values from -5 to -3
Outputs:
- image_loss: float32 [8192], P(('blk', 'grp'))
- image_grad: float32 [8192, 1152], P(('blk', 'grp'))
- text_grad: float32 [8192, 1152], P(('blk', 'grp'))
All inputs are finite; a program needn't handle non-finite values.
Results may differ from a plain program's by a relative error of at most 0.0045.
Values may be sent and summed in bfloat16 or wider, within the bound.
A program may use at most 64 MiB of HBM per device.

v0:
```python
import jax
import jax.numpy as jnp
from jax import lax
from jax.sharding import PartitionSpec as P


def unit_rows(values):
    floats = values.astype(jnp.float32)
    norms = jnp.sqrt(jnp.sum(floats * floats, 1, keepdims=True) + 1e-06)
    return (floats / norms, norms)


def back_rows(grads, units, norms):
    return (grads - units * jnp.sum(units * grads, 1, keepdims=True)) / norms


def local(images, texts, scale, shift):
    rows = images.shape[0]
    image_unit, image_norm = unit_rows(images)
    text_unit, text_norm = unit_rows(texts)
    image_emb = image_unit.astype(jnp.bfloat16)
    text_emb = text_unit.astype(jnp.bfloat16)
    groups = lax.axis_size("grp")
    loops = lax.axis_size("blk")
    total = loops * groups * rows
    gathered = lax.all_gather(image_emb, "grp", axis=0, tiled=True)
    seen = lax.all_gather(text_emb, "blk", axis=0, tiled=True)
    place = lax.axis_index("grp")
    here = lax.axis_index("blk")
    image_ids = jnp.arange(groups * rows, dtype=jnp.int32)[:, None]
    column_ids = place * rows + (jnp.arange(loops * rows, dtype=jnp.int32) % rows)[None, :]
    column_blk = (jnp.arange(loops * rows, dtype=jnp.int32) // rows)[None, :]
    label = ((image_ids == column_ids) & (column_blk == here)).astype(jnp.float32)
    logit = (
        scale
        * lax.dot_general(
            gathered, seen, (((1,), (1,)), ((), ())), preferred_element_type=jnp.float32
        )
        + shift
    )
    loss = jnp.sum(jax.nn.softplus(logit * (1.0 - 2.0 * label)), 1) / total
    coef = ((jax.nn.sigmoid(logit) - label) * scale).astype(jnp.bfloat16)
    image_part = jnp.dot(coef, seen, preferred_element_type=jnp.float32)
    text_part = lax.dot_general(
        coef, gathered, (((0,), (0,)), ((), ())), preferred_element_type=jnp.float32
    )
    image_sum = lax.psum_scatter(image_part, "grp", scatter_dimension=0, tiled=True)
    image_loss = lax.psum_scatter(loss, "grp", scatter_dimension=0, tiled=True)
    text_sum = lax.psum_scatter(text_part, "blk", scatter_dimension=0, tiled=True)
    image_grad = back_rows(image_sum, image_unit, image_norm)
    text_grad = back_rows(text_sum, text_unit, text_norm)
    return (image_loss, image_grad, text_grad)


def solution(mesh):
    in_specs = (P(("blk", "grp"), None), P(("blk", "grp"), None), P(), P())
    out_specs = (P(("blk", "grp")), P(("blk", "grp"), None), P(("blk", "grp"), None))
    return jax.shard_map(local, mesh=mesh, in_specs=in_specs, out_specs=out_specs, check_vma=False)
```

profile of v0, /device:TPU:4, one launch (start us, length us, event | category | flops | bytes accessed | tf_op | source)
XLA Modules:
  0.0 706.1 jit_solution(12393039619672209299)
XLA Ops:
  7.2 0.0 all-gather.2.cloned.1.call-start
  7.2 0.9 fusion.3
  8.1 1.5 fusion.7
  9.6 0.0 all-gather.2.cloned.1.call-update
  9.6 0.0 reduce-scatter.5.cloned.1.call-start
  11.0 0.9 fusion.4
  11.9 0.9 fusion.8
  12.7 70.1 %all_gather.7 = bf16[128,1152]{1,0:T(8,128)(2,1)S(1)} all-gather(bf16[16,1152]{1,0:T(8,128)(2,1)S(1)} %fusion.8), channel_id=1, replica_groups=mesh['blk'=8,'grp'=64] {'blk'}, dimensions={0}, use_global_device_ids=true | all-gather | bytes 331776 | tf_op jit(solution)/shard_map/all_gather | solution.py:27
  82.8 59.4 %all-gather.2.cloned.1.call-done = bf16[1024,1152]{1,0:T(8,128)(2,1)} async-done(((bf16[16,1152]{1,0:T(8,128)(2,1)}), bf16[1024,1152]{1,0:T(8,128)(2,1)}) %all-gather.2.cloned.1.call-update) | async-done | bytes 2359312 | tf_op jit(solution)/shard_map/all_gather | solution.py:26
  142.2 3.0 fusion.1
  145.2 0.0 copy-done.2
  145.2 1.5 fusion.9
  146.7 0.0 reduce-scatter.5.cloned.1.call-update
  146.7 0.0 reduce-scatter.3.cloned.1.call-start
  146.8 3.1 fusion.10
  149.9 0.0 reduce-scatter.3.cloned.1.call-update
  149.9 1.3 dynamic-slice
  151.8 216.2 %all-reduce = f32[1024]{0:T(1024)S(1)} all-reduce(f32[1024]{0:T(1024)S(1)} %broadcast_multiply_fusion), channel_id=2, replica_groups=mesh['blk'=8,'grp'=64] {'grp'}, use_global_device_ids=true, to_apply=%region_3.4.clone | all-reduce | flops 1024 | bytes 8192
  368.0 0.6 dynamic-slice.1
  368.6 1.1 multiply_reduce_fusion
  369.6 1.6 subtract_divide_fusion
  371.2 325.6 %reduce-scatter.3.cloned.1.call-done = f32[16,1152]{1,0:T(8,128)} async-done(((f32[1024,1152]{1,0:T(8,128)}), f32[16,1152]{1,0:T(8,128)}) %reduce-scatter.3.cloned.1.call-update) | async-done | bytes 73744 | tf_op jit(solution)/shard_map/reduce_scatter | solution.py:47
  696.9 1.1 multiply_reduce_fusion.1
  698.0 1.6 subtract_divide_fusion.1
  (11 shorter events, 0.0 us)
Async XLA Ops:
  7.2 135.1 %all-gather.2.cloned.1.call-start = ((), (), s32[]{:S(2)}) async-start(), calls=%async_computation.2 | async-start | bytes 2396160 | tf_op jit(solution)/shard_map/all_gather | solution.py:26
  9.6 359.0 %reduce-scatter.5.cloned.1.call-start = ((), (), s32[]{:S(2)}) async-start(), calls=%async_computation.4 | async-start | bytes 663552 | tf_op jit(solution)/shard_map/reduce_scatter | solution.py:49
  142.2 3.0 copy-start.2
  146.7 550.1 %reduce-scatter.3.cloned.1.call-start = ((), (), s32[]{:S(2)}) async-start(), calls=%async_computation.3 | async-start | bytes 4792320 | tf_op jit(solution)/shard_map/reduce_scatter | solution.py:47
  149.9 218.7 %copy-start = (bf16[16,1152]{1,0:T(8,128)(2,1)S(1)}, bf16[16,1152]{1,0:T(8,128)(2,1)}, u32[]{:S(2)}) copy-start(bf16[16,1152]{1,0:T(8,128)(2,1)} %param.5) | copy-start | bytes 110596
  149.9 547.0 %copy-start.1 = (bf16[16,1152]{1,0:T(8,128)(2,1)S(1)}, bf16[16,1152]{1,0:T(8,128)(2,1)}, u32[]{:S(2)}) copy-start(bf16[16,1152]{1,0:T(8,128)(2,1)} %param.4) | copy-start | bytes 110596
Sparse Core Ops, SparseCore 0:
  10.7 131.4 all-gather.1
  146.9 109.8 reduce-scatter.4
  259.6 437.2 reduce-scatter.2
where the time goes:
time: 707 us; the launch traced here: 706 us
  waiting for transfers between devices  385 us (54%)
  blocking collectives  286 us (40%)
  between operations  15.7 us (2%)
  other arithmetic  9.52 us (1%)
  matrix products  7.54 us (1%)
    reduce_scatter x1, waiting for transfers between devices, local(): lax.psum_scatter(image_part, 'grp', scatter_dimension=0, tiled=True)  326 us
    unnamed x1, blocking collectives  216 us
    all_gather x1, blocking collectives, local(): seen = lax.all_gather(text_emb, 'blk', axis=0, tiled=True)  70.1 us
    all_gather x1, waiting for transfers between devices, local(): gathered = lax.all_gather(image_emb, 'grp', axis=0, tiled=True)  59.4 us
  transfers between devices with their start and end apart: 3, of which 2 were waited for; matrix products, arithmetic and copies ran while one was open for 1% of the time, Pallas kernels for 0%

commit v1 on v0

--- a/solution.py
+++ b/solution.py
@@ -23,7 +23,8 @@
     groups = lax.axis_size("grp")
     loops = lax.axis_size("blk")
     total = loops * groups * rows
-    gathered = lax.all_gather(image_emb, "grp", axis=0, tiled=True)
+    outgoing = jnp.stack([image_emb] * lax.axis_size("grp"))
+    gathered = jnp.concatenate(lax.all_to_all(outgoing, "grp", 0, 0), axis=0)
     seen = lax.all_gather(text_emb, "blk", axis=0, tiled=True)
     place = lax.axis_index("grp")
     here = lax.axis_index("blk")

time: 707 us -> 755 us (1.068)
  blocking collectives: 286 us -> 340 us
  waiting for transfers between devices: 385 us -> 366 us
  starting transfers between devices: 0.12 us -> 16.4 us
    all_gather x1 -> x0, waiting for transfers between devices: 59.4 us -> none  [local(): gathered = lax.all_gather(image_emb, 'grp', axis=0, tiled=True)]
    all_gather x1, blocking collectives: 70.1 us -> 102 us  [local(): seen = lax.all_gather(text_emb, 'blk', axis=0, tiled=True)]
    reduce_scatter x1, waiting for transfers between devices: 326 us -> 348 us  [local(): lax.psum_scatter(image_part, 'grp', scatter_dimension=0, tiled=True)]
    unnamed x1, blocking collectives: 216 us -> 238 us
    all_to_all x0 -> x1, waiting for transfers between devices: none -> 17.6 us  [local(): gathered = jnp.concatenate(lax.all_to_all(outgoing, 'grp', 0, 0), axis=0)]
    all_to_all x0 -> x1, starting transfers between devices: none -> 16.3 us  [local(): gathered = jnp.concatenate(lax.all_to_all(outgoing, 'grp', 0, 0), axis=0)]
where the time goes in v1:
time: 755 us; the launch traced here: 754 us
  waiting for transfers between devices  366 us (48%)
  blocking collectives  340 us (45%)
  starting transfers between devices  16.4 us (2%)
  between operations  16 us (2%)
    reduce_scatter x1, waiting for transfers between devices, local(): lax.psum_scatter(image_part, 'grp', scatter_dimension=0, tiled=True)  348 us
    unnamed x1, blocking collectives  238 us
    all_gather x1, blocking collectives, local(): seen = lax.all_gather(text_emb, 'blk', axis=0, tiled=True)  102 us
    all_to_all x1, waiting for transfers between devices, local(): gathered = jnp.concatenate(lax.all_to_all(outgoing, 'grp', 0, 0), axis=0)  17.6 us
    all_to_all x1, starting transfers between devices, local(): gathered = jnp.concatenate(lax.all_to_all(outgoing, 'grp', 0, 0), axis=0)  16.3 us
  transfers between devices with their start and end apart: 3, of which 2 were waited for; matrix products, arithmetic and copies ran while one was open for 1% of the time, Pallas kernels for 0%

profile of v1, /device:TPU:4, one launch (start us, length us, event | category | flops | bytes accessed | tf_op | source)
XLA Modules:
  0.0 754.4 jit_solution(5277753915352912226)
XLA Ops:
  7.2 0.9 fusion.3
  8.1 0.9 fusion.7
  8.9 1.6 stack.2
  10.5 16.3 %all-to-all-start = ((bf16[64,16,1152]{2,1,0:T(8,128)(2,1)}), bf16[64,16,1152]{2,1,0:T(8,128)(2,1)S(1)}, u32[]{:S(2)}, u32[]{:S(2)}) async-start(bf16[64,16,1152]{2,1,0:T(8,128)(2,1)} %stack.2), calls=%async_computation | async-start | bytes 4718592 | tf_op jit(solution)/shard_map/all_to_all | solution.py:27
  26.8 0.0 reduce-scatter.5.cloned.1.call-start
  28.2 0.0 copy-done
  28.2 0.1 fusion.4
  28.3 0.1 fusion.8
  28.4 101.9 %all_gather.3 = bf16[128,1152]{1,0:T(8,128)(2,1)S(1)} all-gather(bf16[16,1152]{1,0:T(8,128)(2,1)S(1)} %fusion.8), channel_id=1, replica_groups=mesh['blk'=8,'grp'=64] {'blk'}, dimensions={0}, use_global_device_ids=true | all-gather | bytes 331776 | tf_op jit(solution)/shard_map/all_gather | solution.py:28
  130.3 17.6 %all-to-all-done = bf16[64,16,1152]{2,1,0:T(8,128)(2,1)S(1)} async-done(((bf16[64,16,1152]{2,1,0:T(8,128)(2,1)}), bf16[64,16,1152]{2,1,0:T(8,128)(2,1)S(1)}, u32[]{:S(2)}, u32[]{:S(2)}) %all-to-all-start) | async-done | bytes 2359328 | tf_op jit(solution)/shard_map/all_to_all | solution.py:27
  147.9 1.2 fusion.1
  149.1 1.5 fusion.9
  150.5 0.0 reduce-scatter.5.cloned.1.call-update
  150.6 0.0 reduce-scatter.3.cloned.1.call-start
  150.6 3.1 fusion.10
  153.7 0.0 reduce-scatter.3.cloned.1.call-update
  153.7 1.3 dynamic-slice
  155.6 237.8 %all-reduce = f32[1024]{0:T(1024)S(1)} all-reduce(f32[1024]{0:T(1024)S(1)} %broadcast_multiply_fusion), channel_id=2, replica_groups=mesh['blk'=8,'grp'=64] {'grp'}, use_global_device_ids=true, to_apply=%region_3.4.clone | all-reduce | flops 1024 | bytes 8192
  393.5 0.6 dynamic-slice.1
  394.1 1.1 multiply_reduce_fusion
  395.1 1.6 subtract_divide_fusion
  396.8 348.1 %reduce-scatter.3.cloned.1.call-done = f32[16,1152]{1,0:T(8,128)} async-done(((f32[1024,1152]{1,0:T(8,128)}), f32[16,1152]{1,0:T(8,128)}) %reduce-scatter.3.cloned.1.call-update) | async-done | bytes 73744 | tf_op jit(solution)/shard_map/reduce_scatter | solution.py:48
  744.9 1.1 multiply_reduce_fusion.1
  746.0 1.6 subtract_divide_fusion.1
  (9 shorter events, 0.0 us)
Async XLA Ops:
  10.5 17.7 %copy-start = (bf16[16,1152]{1,0:T(8,128)(2,1)S(1)}, bf16[16,1152]{1,0:T(8,128)(2,1)}, u32[]{:S(2)}) copy-start(bf16[16,1152]{1,0:T(8,128)(2,1)} %param.5) | copy-start | bytes 110596
  10.5 137.4 %all-to-all-start = ((bf16[64,16,1152]{2,1,0:T(8,128)(2,1)}), bf16[64,16,1152]{2,1,0:T(8,128)(2,1)S(1)}, u32[]{:S(2)}, u32[]{:S(2)}) async-start(bf16[64,16,1152]{2,1,0:T(8,128)(2,1)} %stack.2), calls=%async_computation | async-start | bytes 4718592 | tf_op jit(solution)/shard_map/all_to_all | solution.py:27
  26.8 367.3 %reduce-scatter.5.cloned.1.call-start = ((), (), s32[]{:S(2)}) async-start(), calls=%async_computation.4 | async-start | bytes 663552 | tf_op jit(solution)/shard_map/reduce_scatter | solution.py:50
  150.6 594.3 %reduce-scatter.3.cloned.1.call-start = ((), (), s32[]{:S(2)}) async-start(), calls=%async_computation.3 | async-start | bytes 4792320 | tf_op jit(solution)/shard_map/reduce_scatter | solution.py:48
  153.7 591.2 %copy-start.1 = (bf16[16,1152]{1,0:T(8,128)(2,1)S(1)}, bf16[16,1152]{1,0:T(8,128)(2,1)}, u32[]{:S(2)}) copy-start(bf16[16,1152]{1,0:T(8,128)(2,1)} %param.4) | copy-start | bytes 110596
Sparse Core Ops, SparseCore 0:
  150.7 153.3 reduce-scatter.4
  306.9 437.9 reduce-scatter.2
